TPU v7x, 128 devices: a whole 4x4x4 slice. The times are simulated.
128 devices in a mesh: ctx: 8 (over x, z_lo), fsdp: 16 (over z_hi, y, core).
Axes of the slice: x: 4, y: 4, z: 4 (z_hi: 2, z_lo: 2; z = z_hi * 2 + z_lo), core: 2. Of those that a mesh axis runs over, the one named last changes fastest.
Arguments:
- inputs: bfloat16 [16, 1024, 1152], P('fsdp', 'ctx'), may hold values from -6 to 6
- out_grad: bfloat16 [16, 1024, 1152], P('fsdp', 'ctx'), may hold values from -6 to 6
- positions: int32 [16, 1024], P('fsdp', 'ctx'), may hold values from 0 to 1023, as said below
- block_order: int32 [8, 2], replicated, may hold values from 0 to 15, as said below
- w_query: bfloat16 [1152, 1024], P('fsdp'), may hold values from -0.1875 to 0.1875
- w_key: bfloat16 [1152, 256], P('fsdp'), may hold values from -0.1875 to 0.1875
- w_value: bfloat16 [1152, 256], P('fsdp'), may hold values from -0.1875 to 0.1875
- w_output: bfloat16 [1024, 1152], P(None, 'fsdp'), may hold values from -0.1875 to 0.1875
- w_gate: bfloat16 [6912, 1152], P('fsdp'), may hold values from -0.1875 to 0.1875
- w_up: bfloat16 [6912, 1152], P('fsdp'), may hold values from -0.1875 to 0.1875
- w_down: bfloat16 [6912, 1152], P('fsdp'), may hold values from -0.078125 to 0.078125
- gain_in: bfloat16 [1152], P('fsdp'), may hold values from 0.099609375 to 1.8984375
- gain_query: bfloat16 [256], P('fsdp'), may hold values from 0.099609375 to 1.8984375
- gain_key: bfloat16 [256], P('fsdp'), may hold values from 0.099609375 to 1.8984375
- gain_attn: bfloat16 [1152], P('fsdp'), may hold values from 0.099609375 to 1.8984375
- gain_pre: bfloat16 [1152], P('fsdp'), may hold values from 0.099609375 to 1.8984375
- gain_post: bfloat16 [1152], P('fsdp'), may hold values from 0.099609375 to 1.8984375
Outputs:
- outputs: bfloat16 [16, 1024, 1152], P('fsdp', 'ctx')
- in_grad: bfloat16 [16, 1024, 1152], P('fsdp', 'ctx')
- grad_w_query: float32 [1152, 1024], P('fsdp')
- grad_w_key: float32 [1152, 256], P('fsdp')
- grad_w_value: float32 [1152, 256], P('fsdp')
- grad_w_output: float32 [1024, 1152], P(None, 'fsdp')
- grad_w_gate: float32 [6912, 1152], P('fsdp')
- grad_w_up: float32 [6912, 1152], P('fsdp')
- grad_w_down: float32 [6912, 1152], P('fsdp')
- grad_gain_in: float32 [1152], P('fsdp')
- grad_gain_query: float32 [256], P('fsdp')
- grad_gain_key: float32 [256], P('fsdp')
- grad_gain_attn: float32 [1152], P('fsdp')
- grad_gain_pre: float32 [1152], P('fsdp')
- grad_gain_post: float32 [1152], P('fsdp')
Inputs may be any that keep to these rules, and one draw needn't show every extreme that they name: `block_order`: row c names the two blocks of 64 tokens in device c's rows, in order; every block appears once, and a row holds blocks k and m with k + m one less than the number of blocks. `positions`: each row's offset from the start of its document in the sequence; documents begin at the sequence's first token and at random places; sequence 0 is one document.
All inputs are finite; a program needn't handle non-finite values.
Results may differ from a plain program's by a relative error of at most 0.03.
Values may be sent and summed in bfloat16 or wider, within the bound.
No kernel may reach another device: no remote copies, remote signals or barrier semaphores. Data moves between devices by JAX's collectives and lax.ppermute only.
A program may use at most 128 MiB of HBM per device.

v0:
```python
import jax
import jax.numpy as jnp
from jax import lax
from jax.sharding import PartitionSpec as P

H = 4
HD = 256
EPS = 1e-06
ROPE_BASE = 1000000.0
GELU_C = 0.7978845608028654
GELU_A = 0.044715


def norm_forward(values, gain):
    inverse = lax.rsqrt(jnp.mean(values * values, axis=-1, keepdims=True) + EPS)
    unit = values * inverse
    return (unit * gain, unit, inverse)


def norm_backward(upstream, unit, inverse, gain):
    scaled = upstream * gain
    inner = jnp.mean(scaled * unit, axis=-1, keepdims=True)
    leading = tuple(range(upstream.ndim - 1))
    return (inverse * (scaled - unit * inner), jnp.sum(upstream * unit, axis=leading))


def gelu_pair(gate):
    inner = GELU_C * (gate + GELU_A * gate * gate * gate)
    tangent = jnp.tanh(inner)
    value = 0.5 * gate * (1.0 + tangent)
    slope = 0.5 * (1.0 + tangent) + 0.5 * gate * (1.0 - tangent * tangent) * GELU_C * (
        1.0 + 3.0 * GELU_A * gate * gate
    )
    return (value, slope)


def rope_tables(positions, width):
    half = width // 2
    freqs = ROPE_BASE ** (-2.0 * jnp.arange(half, dtype=jnp.float32) / width)
    angles = positions.astype(jnp.float32)[:, None] * freqs[None, :]
    return (jnp.cos(angles), jnp.sin(angles))


def rotate(values, cosine, sine):
    half = values.shape[-1] // 2
    first = values[..., :half]
    second = values[..., half:]
    return jnp.concatenate(
        [first * cosine - second * sine, second * cosine + first * sine], axis=-1
    )


def rotate_back(values, cosine, sine):
    half = values.shape[-1] // 2
    first = values[..., :half]
    second = values[..., half:]
    return jnp.concatenate(
        [first * cosine + second * sine, second * cosine - first * sine], axis=-1
    )


def sequence_rows(order_flat, first_row, count, block):
    rows = first_row + jnp.arange(count, dtype=jnp.int32)
    slots = rows // block
    table = jnp.arange(order_flat.shape[0], dtype=jnp.int32)
    picked = jnp.sum(jnp.where(slots[:, None] == table[None, :], order_flat[None, :], 0), axis=1)
    return picked * block + rows % block


def pad_rows(shard, rows):
    return jnp.pad(shard, (0, rows - shard.shape[0]))


def a2a_sum(x, axis_name, count):
    pieces = lax.all_to_all(x.reshape(count, -1, *x.shape[1:]), axis_name, 0, 0)
    return jnp.sum(pieces.astype(jnp.float32), axis=0)


def a2a_gather(x, axis_name, count):
    copies = jnp.broadcast_to(x[None], (count,) + x.shape)
    return lax.all_to_all(copies, axis_name, 0, 0).reshape(count * x.shape[0], *x.shape[1:])


def body(
    inputs,
    out_grad,
    positions,
    block_order,
    w_query,
    w_key,
    w_value,
    w_output,
    w_gate,
    w_up,
    w_down,
    gain_in,
    gain_query,
    gain_key,
    gain_attn,
    gain_pre,
    gain_post,
):
    f32 = jnp.float32
    low = jnp.bfloat16
    tokens = inputs[0]
    local = tokens.shape[0]
    parts = lax.axis_size("ctx")
    groups = lax.axis_size("fsdp")
    total = local * parts
    block = local // 2
    width_shard = w_query.shape[0]
    qw = w_query.shape[1]
    kw = w_key.shape[1]
    gain_cols = jnp.stack(
        [
            gain_in,
            gain_attn,
            gain_pre,
            gain_post,
            pad_rows(gain_query, width_shard),
            pad_rows(gain_key, width_shard),
        ],
        axis=1,
    )
    gain_cols = jnp.pad(gain_cols, ((0, 0), (0, 128 - gain_cols.shape[1])))
    packed = jnp.concatenate([w_query, w_key, w_value, w_output.T, gain_cols], axis=1)
    packed_all = lax.all_gather(packed, "fsdp", axis=0, tiled=True)
    o1 = qw
    o2 = o1 + kw
    o3 = o2 + kw
    o4 = o3 + w_output.shape[0]
    full_query = packed_all[:, :o1]
    full_key = packed_all[:, o1:o2]
    full_value = packed_all[:, o2:o3]
    full_output_t = packed_all[:, o3:o4]
    gains_all = packed_all[:, o4:].astype(f32)
    head_shard = gain_query.shape[0]

    def head_gain(col):
        return col.reshape(groups, width_shard)[:, :head_shard].reshape(-1)

    norm_in = gains_all[:, 0]
    norm_attn = gains_all[:, 1]
    norm_pre = gains_all[:, 2]
    norm_post = gains_all[:, 3]
    norm_query = head_gain(gains_all[:, 4])
    norm_key = head_gain(gains_all[:, 5])
    ctx_index = lax.axis_index("ctx")
    order_flat = block_order.reshape(-1)
    my_seq = sequence_rows(order_flat, ctx_index * local, local, block)
    all_seq = sequence_rows(order_flat, 0, total, block)
    flat_in = tokens.astype(f32)
    normed_full, unit_in, inv_in = norm_forward(flat_in, norm_in)
    normed_in = normed_full.astype(low)
    queries = jnp.dot(normed_in, full_query, preferred_element_type=f32).reshape(local, H, HD)
    keys_raw = jnp.dot(normed_in, full_key, preferred_element_type=f32)
    values = jnp.dot(normed_in, full_value, preferred_element_type=f32).astype(low)
    query_normed, query_unit, query_inv = norm_forward(queries, norm_query)
    key_normed, key_unit, key_inv = norm_forward(keys_raw, norm_key)
    cosine, sine = rope_tables(positions[0], HD)
    scale = HD ** (-0.5)
    query_rot = (rotate(query_normed, cosine[:, None, :], sine[:, None, :]) * scale).astype(low)
    key_rot = rotate(key_normed, cosine, sine).astype(low)
    kv_all = a2a_gather(jnp.concatenate([key_rot, values], axis=1), "ctx", parts)
    key_all = kv_all[:, :HD]
    value_all = kv_all[:, HD:]
    scores = jnp.einsum("qhd,kd->hqk", query_rot, key_all, preferred_element_type=f32)
    allowed = my_seq[:, None] >= all_seq[None, :]
    scores = jnp.where(allowed[None], scores, -jnp.inf)
    highest = jnp.max(scores, axis=-1, keepdims=True)
    log_total = highest + jnp.log(jnp.sum(jnp.exp(scores - highest), axis=-1, keepdims=True))
    probs_full = jnp.exp(scores - log_total)
    probs = probs_full.astype(low)
    attended = (
        jnp.einsum("hqk,kd->qhd", probs, value_all, preferred_element_type=f32)
        .reshape(local, H * HD)
        .astype(low)
    )
    branch_attn = jnp.einsum("tc,dc->td", attended, full_output_t, preferred_element_type=f32)
    attn_normed, attn_unit, attn_inv = norm_forward(branch_attn, norm_attn)
    residual = flat_in + attn_normed
    pre_full, pre_unit, pre_inv = norm_forward(residual, norm_pre)
    normed_pre = pre_full.astype(low)
    rows_all = lax.all_gather(normed_pre, "fsdp", axis=0, tiled=True)
    gate = jnp.einsum("td,fd->tf", rows_all, w_gate, preferred_element_type=f32)
    upper = jnp.einsum("td,fd->tf", rows_all, w_up, preferred_element_type=f32)
    gelu_value, gelu_slope = gelu_pair(gate)
    hidden = (gelu_value * upper).astype(low)
    branch_ffn = a2a_sum(
        jnp.dot(hidden, w_down, preferred_element_type=f32).astype(jnp.bfloat16), "fsdp", groups
    )
    post_normed, post_unit, post_inv = norm_forward(branch_ffn, norm_post)
    outputs = (residual + post_normed).astype(low)
    grad_out = out_grad[0].astype(f32)
    grad_ffn_full, grad_gain_post = norm_backward(grad_out, post_unit, post_inv, norm_post)
    grad_ffn = grad_ffn_full.astype(low)
    grad_all = a2a_gather(grad_ffn, "fsdp", groups)
    grad_hidden = jnp.einsum("td,fd->tf", grad_all, w_down, preferred_element_type=f32)
    grad_gate = (grad_hidden * upper * gelu_slope).astype(low)
    grad_up = (grad_hidden * gelu_value).astype(low)
    shard_gate = jnp.einsum("tf,td->fd", grad_gate, rows_all, preferred_element_type=f32)
    shard_up = jnp.einsum("tf,td->fd", grad_up, rows_all, preferred_element_type=f32)
    shard_down = jnp.einsum("tf,td->fd", hidden, grad_all, preferred_element_type=f32)
    grad_pre = a2a_sum(
        (
            jnp.dot(grad_gate, w_gate, preferred_element_type=f32)
            + jnp.dot(grad_up, w_up, preferred_element_type=f32)
        ).astype(jnp.bfloat16),
        "fsdp",
        groups,
    )
    grad_from_pre, grad_gain_pre = norm_backward(grad_pre, pre_unit, pre_inv, norm_pre)
    grad_residual = grad_out + grad_from_pre
    grad_branch_full, grad_gain_attn = norm_backward(grad_residual, attn_unit, attn_inv, norm_attn)
    grad_branch = grad_branch_full.astype(low)
    term_output = jnp.einsum("tc,td->cd", attended, grad_branch, preferred_element_type=f32)
    grad_attended = jnp.einsum(
        "td,dc->tc", grad_branch, full_output_t, preferred_element_type=f32
    ).astype(low)
    grad_heads = grad_attended.reshape(local, H, HD)
    attended_heads = attended.reshape(local, H, HD)
    delta = jnp.transpose(jnp.sum(grad_heads.astype(f32) * attended_heads.astype(f32), axis=-1))[
        :, :, None
    ]
    grad_probs = jnp.einsum("qhd,kd->hqk", grad_heads, value_all, preferred_element_type=f32)
    grad_scores = (probs_full * (grad_probs - delta)).astype(low)
    value_term = jnp.einsum("hqk,qhd->kd", probs, grad_heads, preferred_element_type=f32)
    key_term = jnp.einsum("hqk,qhd->kd", grad_scores, query_rot, preferred_element_type=f32)
    key_value_terms = jnp.concatenate([key_term, value_term], axis=1)
    grad_query_rot = jnp.einsum("hqk,kd->qhd", grad_scores, key_all, preferred_element_type=f32)
    summed_kv = a2a_sum(key_value_terms.astype(jnp.bfloat16), "ctx", parts)
    grad_key_rot = summed_kv[:, :HD]
    grad_values = summed_kv[:, HD:].astype(low)
    grad_q_normed = rotate_back(grad_query_rot * scale, cosine[:, None, :], sine[:, None, :])
    grad_q_full, grad_gain_query = norm_backward(grad_q_normed, query_unit, query_inv, norm_query)
    grad_k_normed = rotate_back(grad_key_rot, cosine, sine)
    grad_k_full, grad_gain_key = norm_backward(grad_k_normed, key_unit, key_inv, norm_key)
    grad_q_in = grad_q_full.reshape(local, H * HD).astype(low)
    grad_k_in = grad_k_full.astype(low)
    term_query = jnp.einsum("tc,td->cd", grad_q_in, normed_in, preferred_element_type=f32)
    term_key = jnp.einsum("tc,td->cd", grad_k_in, normed_in, preferred_element_type=f32)
    term_value = jnp.einsum("tc,td->cd", grad_values, normed_in, preferred_element_type=f32)
    grad_normed = (
        jnp.einsum("tc,dc->td", grad_q_in, full_query, preferred_element_type=f32)
        + jnp.einsum("tc,dc->td", grad_k_in, full_key, preferred_element_type=f32)
        + jnp.einsum("tc,dc->td", grad_values, full_value, preferred_element_type=f32)
    )
    grad_from_in, grad_gain_in = norm_backward(grad_normed, unit_in, inv_in, norm_in)
    in_grad = (grad_residual + grad_from_in).astype(low)

    def head_col(g):
        return jnp.pad(
            g.reshape(groups, head_shard), ((0, 0), (0, width_shard - head_shard))
        ).reshape(-1)

    gain_block = jnp.stack(
        [
            grad_gain_in,
            grad_gain_attn,
            grad_gain_pre,
            grad_gain_post,
            head_col(grad_gain_query),
            head_col(grad_gain_key),
        ],
        axis=0,
    )
    gain_block = jnp.pad(gain_block, ((0, 8 - gain_block.shape[0]), (0, 0))).astype(low)
    gain_block = jnp.transpose(gain_block.reshape(8, groups, width_shard), (1, 0, 2))
    gain_shard = jnp.sum(lax.all_to_all(gain_block, "fsdp", 0, 0).astype(f32), axis=0)

    def ctx_sum(x):
        chunks = x.reshape(parts, -1, x.shape[1])
        mine = jnp.sum(lax.all_to_all(chunks, "ctx", 0, 0).astype(f32), axis=0).astype(low)
        return lax.all_to_all(jnp.broadcast_to(mine[None], chunks.shape), "ctx", 0, 0).reshape(
            x.shape
        )

    ffn_units = shard_gate.shape[0]
    ffn_sums = ctx_sum(
        jnp.concatenate([shard_gate, shard_up, shard_down], axis=0).astype(low)
    ).astype(f32)
    grad_packed = jnp.concatenate([term_query, term_key, term_value, term_output], axis=0).astype(
        low
    )
    grad_shard = jnp.concatenate(
        [
            lax.psum_scatter(grad_packed, "fsdp", scatter_dimension=1, tiled=True),
            gain_shard.astype(low),
        ],
        axis=0,
    )
    totals = (
        ctx_sum(grad_shard),
        ffn_sums[:ffn_units],
        ffn_sums[ffn_units : 2 * ffn_units],
        ffn_sums[2 * ffn_units :],
    )
    grad_shard = totals[0].astype(f32)
    grows = grad_shard[o4:]
    return (
        outputs[None],
        in_grad[None],
        grad_shard[:o1].T,
        grad_shard[o1:o2].T,
        grad_shard[o2:o3].T,
        grad_shard[o3:o4],
        totals[1].astype(f32),
        totals[2].astype(f32),
        totals[3].astype(f32),
        grows[0],
        grows[4, :head_shard],
        grows[5, :head_shard],
        grows[1],
        grows[2],
        grows[3],
    )


def solution(mesh):
    placed = (
        P("fsdp", "ctx", None),
        P("fsdp", "ctx", None),
        P("fsdp", "ctx"),
        P(),
        P("fsdp", None),
        P("fsdp", None),
        P("fsdp", None),
        P(None, "fsdp"),
        P("fsdp", None),
        P("fsdp", None),
        P("fsdp", None),
        P("fsdp"),
        P("fsdp"),
        P("fsdp"),
        P("fsdp"),
        P("fsdp"),
        P("fsdp"),
    )
    return jax.shard_map(
        body,
        mesh=mesh,
        in_specs=placed,
        out_specs=(
            P("fsdp", "ctx", None),
            P("fsdp", "ctx", None),
            P("fsdp", None),
            P("fsdp", None),
            P("fsdp", None),
            P(None, "fsdp"),
            P("fsdp", None),
            P("fsdp", None),
            P("fsdp", None),
            P("fsdp"),
            P("fsdp"),
            P("fsdp"),
            P("fsdp"),
            P("fsdp"),
            P("fsdp"),
        ),
        check_vma=False,
    )
```

profile of v0, /device:TPU:0, one launch (start us, length us, event | category | flops | bytes accessed | tf_op | source)
XLA Modules:
  0.0 611.8 jit_solution(8419735347400589756)
XLA Ops:
  16.2 63.4 %all-gather.3.cloned.1.call-done = bf16[1152,2688]{1,0:T(8,128)(2,1)} async-done(((bf16[72,2688]{1,0:T(8,128)(2,1)}), bf16[1152,2688]{1,0:T(8,128)(2,1)}) %all-gather.3.cloned.1.call-update) | async-done | bytes 6193168 | tf_op jit(solution)/shard_map/all_gather | solution.py:127
  87.3 4.3 copy.90
  94.8 4.3 all-to-all-start
  103.4 12.4 %all-to-all-done = bf16[8,128,512]{2,1,0:T(8,128)(2,1)S(1)} async-done(((bf16[8,128,512]{2,1,0:T(8,128)(2,1)}), bf16[8,128,512]{2,1,0:T(8,128)(2,1)S(1)}, u32[]{:S(2)}, u32[]{:S(2)}) %all-to-all-start) | async-done | bytes 1048608 | tf_op jit(solution)/shard_map/all_to_all | solution.py:81
  122.3 54.8 %all-gather.5.cloned.1.call-done = bf16[2048,1152]{1,0:T(8,128)(2,1)} async-done(((bf16[128,1152]{1,0:T(8,128)(2,1)}), bf16[2048,1152]{1,0:T(8,128)(2,1)}) %all-gather.5.cloned.1.call-update) | async-done | bytes 4718608 | tf_op jit(solution)/shard_map/all_gather | solution.py:184
  177.1 5.2 fusion.109
  188.5 60.9 %all_to_all.50 = bf16[16,128,1152]{2,1,0:T(8,128)(2,1)S(1)} all-to-all(bf16[16,128,1152]{2,1,0:T(8,128)(2,1)S(1)} %bitcast.206), channel_id=1, replica_groups=mesh['ctx'=8,'fsdp'=16] {'fsdp'}, dimensions={0} | all-to-all | bytes 9437184 | tf_op jit(solution)/shard_map/all_to_all | solution.py:75
  252.2 60.2 %all_to_all.51 = bf16[16,128,1152]{2,1,0:T(8,128)(2,1)S(1)} all-to-all(bf16[16,128,1152]{2,1,0:T(8,128)(2,1)S(1)} %broadcast_in_dim.66), channel_id=1, replica_groups=mesh['ctx'=8,'fsdp'=16] {'fsdp'}, dimensions={0} | all-to-all | bytes 9437184 | tf_op jit(solution)/shard_map/all_to_all | solution.py:81
  312.4 4.6 multiply_convert_fusion
  320.0 4.8 add_convert_fusion
  324.8 4.6 all-to-all-start.3
  332.6 60.1 %all-to-all-done.3 = bf16[16,128,1152]{2,1,0:T(8,128)(2,1)} async-done(((bf16[16,128,1152]{2,1,0:T(8,128)(2,1)}), bf16[16,128,1152]{2,1,0:T(8,128)(2,1)}, u32[]{:S(2)}, u32[]{:S(2)}) %all-to-all-start.3) | async-done | bytes 4718624 | tf_op jit(solution)/shard_map/all_to_all | solution.py:75
  409.2 5.2 all-to-all-start.4
  422.7 7.5 %all-to-all-done.4 = bf16[8,128,512]{2,1,0:T(8,128)(2,1)S(1)} async-done(((bf16[8,128,512]{2,1,0:T(8,128)(2,1)}), bf16[8,128,512]{2,1,0:T(8,128)(2,1)S(1)}, u32[]{:S(2)}, u32[]{:S(2)}) %all-to-all-start.4) | async-done | bytes 1048608 | tf_op jit(solution)/shard_map/all_to_all | solution.py:75
  431.8 4.6 pad_maximum_fusion
  436.5 8.9 %copy.117 = bf16[2560,1152]{0,1:T(8,128)(2,1)} copy(bf16[2560,1152]{1,0:T(8,128)(2,1)} %pad_maximum_fusion) | data formatting | bytes 11796480
  445.4 5.5 convolution_convert_fusion.3
  461.3 44.3 %all_to_all.52 = bf16[8,162,1152]{2,1,0:T(8,128)(2,1)} all-to-all(bf16[8,162,1152]{2,1,0:T(8,128)(2,1)} %convert_element_type.207), channel_id=1, replica_groups=mesh['ctx'=8,'fsdp'=16] {'ctx'}, dimensions={0} | all-to-all | bytes 5971968 | tf_op jit(solution)/shard_map/all_to_all | solution.py:273
  509.9 5.1 all-to-all-start.9
  521.9 35.5 %all-to-all-done.9 = bf16[8,162,1152]{2,1,0:T(8,128)(2,1)} async-done(((bf16[8,162,1152]{2,1,0:T(8,128)(2,1)}), bf16[8,162,1152]{2,1,0:T(8,128)(2,1)}, u32[]{:S(2)}, u32[]{:S(2)}) %all-to-all-start.9) | async-done | bytes 2986016 | tf_op jit(solution)/shard_map/all_to_all | solution.py:274
  557.4 8.7 %all-to-all-start.5 = ((bf16[16,8,72]{2,1,0:T(8,128)(2,1)}), bf16[16,8,72]{2,1,0:T(8,128)(2,1)S(1)}, u32[]{:S(2)}, u32[]{:S(2)}) async-start(bf16[16,8,72]{2,1,0:T(8,128)(2,1)} %copy.100), calls=%async_computation.5 | async-start | bytes 65536 | tf_op jit(solution)/shard_map/all_to_all | solution.py:269
  566.1 4.3 reshape.425
  579.9 5.5 fusion.107
  594.3 7.4 %all-to-all-done.7 = bf16[8,321,72]{1,2,0:T(8,128)(2,1)S(1)} async-done(((bf16[8,321,72]{1,2,0:T(8,128)(2,1)}), bf16[8,321,72]{1,2,0:T(8,128)(2,1)S(1)}, u32[]{:S(2)}, u32[]{:S(2)}) %all-to-all-start.7) | async-done | bytes 369824 | tf_op jit(solution)/shard_map/all_to_all | solution.py:274
  (236 shorter events, 114.5 us)
Async XLA Ops:
  7.2 178.1 %copy-start = (bf16[432,1152]{1,0:T(8,128)(2,1)S(1)}, bf16[432,1152]{1,0:T(8,128)(2,1)}, u32[]{:S(2)}) copy-start(bf16[432,1152]{1,0:T(8,128)(2,1)} %param.27) | copy-start | bytes 2985988
  7.2 75.2 %copy-start.2 = (bf16[1,128,1152]{2,1,0:T(8,128)(2,1)S(1)}, bf16[1,128,1152]{2,1,0:T(8,128)(2,1)}, u32[]{:S(2)}) copy-start(bf16[1,128,1152]{2,1,0:T(8,128)(2,1)} %param.17) | copy-start | bytes 884740
  7.2 72.4 %all-gather.3.cloned.1.call-start = ((), (), s32[]{:S(2)}) async-start(), calls=%async_computation.11 | async-start | bytes 6580224 | tf_op jit(solution)/shard_map/all_gather | solution.py:127
  13.9 78.0 %copy-start.35 = (f32[128]{0:T(128)}, f32[128]{0:T(128)S(1)}, u32[]{:S(2)}) copy-start(f32[128]{0:T(128)S(1)} %multiply_power_fusion) | copy-start | bytes 1540
  15.9 76.0 %copy-start.37 = (f32[128]{0:T(128)}, f32[128]{0:T(128)S(1)}, u32[]{:S(2)}) copy-start(f32[128]{0:T(128)S(1)} %convert_bitcast_fusion.2) | copy-start | bytes 1540
  16.2 100.7 %copy-start.25 = (pred[128,1024]{0,1:T(8,128)(4,1)}, pred[128,1024]{0,1:T(8,128)(4,1)S(1)}, u32[]{:S(2)}) copy-start(pred[128,1024]{0,1:T(8,128)(4,1)S(1)} %broadcast_compare_fusion.1) | copy-start | bytes 393220
  94.8 21.1 %all-to-all-start = ((bf16[8,128,512]{2,1,0:T(8,128)(2,1)}), bf16[8,128,512]{2,1,0:T(8,128)(2,1)S(1)}, u32[]{:S(2)}, u32[]{:S(2)}) async-start(bf16[8,128,512]{2,1,0:T(8,128)(2,1)} %broadcast_in_dim.56), calls=%async_computation | async-start | bytes 2097152 | tf_op jit(solution)/shard_map/all_to_all | solution.py:81
  99.1 77.9 %all-gather.5.cloned.1.call-start = ((), (), s32[]{:S(2)}) async-start(), calls=%async_computation.12 | async-start | bytes 5013504 | tf_op jit(solution)/shard_map/all_gather | solution.py:184
  103.4 13.4 %copy-start.26 = (f32[128,4,128]{2,0,1:T(8,128)}, f32[128,4,128]{2,0,1:T(8,128)S(1)}, u32[]{:S(2)}) copy-start(f32[128,4,128]{2,0,1:T(8,128)S(1)} %get-tuple-element.53) | copy-start | bytes 786436
  103.4 14.9 %copy-start.28 = (f32[128,4,128]{2,0,1:T(8,128)}, f32[128,4,128]{2,0,1:T(8,128)S(1)}, u32[]{:S(2)}) copy-start(f32[128,4,128]{2,0,1:T(8,128)S(1)} %get-tuple-element.54) | copy-start | bytes 786436
  117.7 211.9 %copy-start.30 = (f32[4,128]{1,0:T(4,128)}, f32[4,128]{1,0:T(4,128)S(1)}, u32[]{:S(2)}) copy-start(f32[4,128]{1,0:T(4,128)S(1)} %log_add_fusion) | copy-start | bytes 6148
  118.3 64.0 %copy-start.16 = (bf16[256,4,128]{2,0,1:T(8,128)(2,1)}, bf16[256,4,128]{2,0,1:T(8,128)(2,1)S(1)}, u32[]{:S(2)}) copy-start(bf16[256,4,128]{2,0,1:T(8,128)(2,1)S(1)} %convolution_convert_fusion.8) | copy-start | bytes 786436
  121.1 274.9 %copy-start.10 = (f32[128,1152]{1,0:T(8,128)}, f32[128,1152]{1,0:T(8,128)S(1)}, u32[]{:S(2)}) copy-start(f32[128,1152]{1,0:T(8,128)S(1)} %get-tuple-element.71) | copy-start | bytes 1769476
  121.1 274.9 %copy-start.32 = (f32[128]{0:T(128)}, f32[128]{0:T(128)S(1)}, u32[]{:S(2)}) copy-start(f32[128]{0:T(128)S(1)} %add_rsqrt_fusion.3) | copy-start | bytes 1540
  324.8 67.9 %all-to-all-start.3 = ((bf16[16,128,1152]{2,1,0:T(8,128)(2,1)}), bf16[16,128,1152]{2,1,0:T(8,128)(2,1)}, u32[]{:S(2)}, u32[]{:S(2)}) async-start(bf16[16,128,1152]{2,1,0:T(8,128)(2,1)} %bitcast.205), calls=%async_computation.3 | async-start | bytes 9437184 | tf_op jit(solution)/shard_map/all_to_all | solution.py:75
  409.2 21.0 %all-to-all-start.4 = ((bf16[8,128,512]{2,1,0:T(8,128)(2,1)}), bf16[8,128,512]{2,1,0:T(8,128)(2,1)S(1)}, u32[]{:S(2)}, u32[]{:S(2)}) async-start(bf16[8,128,512]{2,1,0:T(8,128)(2,1)} %pad_maximum_fusion.2), calls=%async_computation.4 | async-start | bytes 2097152 | tf_op jit(solution)/shard_map/all_to_all | solution.py:75
  414.4 159.4 %reduce-scatter.4.cloned.1.call-start = ((), (), s32[]{:S(2)}) async-start(), calls=%async_computation.13 | async-start | bytes 6266880
  418.1 12.9 %copy-start.34 = (f32[128]{0:T(128)S(1)}, f32[128]{0:T(128)}, u32[]{:S(2)}) copy-start(f32[128]{0:T(128)} %copy-done.33) | copy-start | bytes 1540
  509.9 47.5 %all-to-all-start.9 = ((bf16[8,162,1152]{2,1,0:T(8,128)(2,1)}), bf16[8,162,1152]{2,1,0:T(8,128)(2,1)}, u32[]{:S(2)}, u32[]{:S(2)}) async-start(bf16[8,162,1152]{2,1,0:T(8,128)(2,1)} %broadcast_in_dim.117), calls=%async_computation.9 | async-start | bytes 6193152 | tf_op jit(solution)/shard_map/all_to_all | solution.py:274
  557.4 16.3 %all-to-all-start.5 = ((bf16[16,8,72]{2,1,0:T(8,128)(2,1)}), bf16[16,8,72]{2,1,0:T(8,128)(2,1)S(1)}, u32[]{:S(2)}, u32[]{:S(2)}) async-start(bf16[16,8,72]{2,1,0:T(8,128)(2,1)} %copy.100), calls=%async_computation.5 | async-start | bytes 65536 | tf_op jit(solution)/shard_map/all_to_all | solution.py:269
  576.4 12.5 %all-to-all-start.6 = ((bf16[8,321,72]{1,2,0:T(8,128)(2,1)}), bf16[8,321,72]{1,2,0:T(8,128)(2,1)S(1)}, u32[]{:S(2)}, u32[]{:S(2)}) async-start(bf16[8,321,72]{1,2,0:T(8,128)(2,1)} %copy.102), calls=%async_computation.6 | async-start | bytes 884736 | tf_op jit(solution)/shard_map/all_to_all | solution.py:273
  579.8 13.4 %copy-start.9 = (f32[128,1152]{1,0:T(8,128)S(1)}, f32[128,1152]{1,0:T(8,128)}, u32[]{:S(2)}) copy-start(f32[128,1152]{1,0:T(8,128)} %copy-done.8) | copy-start | bytes 1769476
  589.0 16.0 %copy-start.1 = (bf16[432,1152]{1,0:T(8,128)(2,1)S(1)}, bf16[432,1152]{1,0:T(8,128)(2,1)}, u32[]{:S(2)}) copy-start(bf16[432,1152]{1,0:T(8,128)(2,1)} %param.27) | copy-start | bytes 2985988
  589.8 11.9 %all-to-all-start.7 = ((bf16[8,321,72]{1,2,0:T(8,128)(2,1)}), bf16[8,321,72]{1,2,0:T(8,128)(2,1)S(1)}, u32[]{:S(2)}, u32[]{:S(2)}) async-start(bf16[8,321,72]{1,2,0:T(8,128)(2,1)} %broadcast_in_dim.116), calls=%async_computation.7 | async-start | bytes 884736 | tf_op jit(solution)/shard_map/all_to_all | solution.py:274
  (35 other events, 187.4 us)
Sparse Core Ops, SparseCore 0:
  13.2 66.3 all-gather.2
  122.4 54.6 all-gather.4
  445.5 122.8 reduce-scatter.3
where the time goes:
time: 617 us; the launch traced here: 612 us
  waiting for transfers between devices  248 us (40%)
  blocking collectives  165 us (27%)
  matrix products  61.3 us (10%)
  local copies, waits for them, and re-layouts  55.1 us (9%)
  starting transfers between devices  35.7 us (6%)
  other arithmetic  31.1 us (5%)
  between operations  15.1 us (2%)
    all_to_all x2, waiting for transfers between devices, a2a_sum(): pieces = lax.all_to_all(x.reshape(count, -1, *x.shape[1:]), axis_name, 0, 0)  67.6 us
    all_gather x1, waiting for transfers between devices, body(): packed_all = lax.all_gather(packed, 'fsdp', axis=0, tiled=True)  63.4 us
    all_to_all x1, blocking collectives, a2a_sum(): pieces = lax.all_to_all(x.reshape(count, -1, *x.shape[1:]), axis_name, 0, 0)  60.9 us
    all_to_all x1, blocking collectives, a2a_gather(): lax.all_to_all(copies, axis_name, 0, 0)  60.2 us
    all_gather x1, waiting for transfers between devices, body(): rows_all = lax.all_gather(normed_pre, 'fsdp', axis=0, tiled=True)  54.8 us
    all_to_all x1, blocking collectives, ctx_sum(): lax.all_to_all(chunks, 'ctx', 0, 0).astype(f32)  44.3 us
    all_to_all x2, waiting for transfers between devices, ctx_sum(): lax.all_to_all(jnp.broadcast_to(mine[None], chunks.shape), 'ctx', 0, 0)  43 us
    unnamed x106, local copies, waits for them, and re-layouts  18 us
  transfers between devices with their start and end apart: 10, of which 9 were waited for; matrix products, arithmetic and copies ran while one was open for 9% of the time, Pallas kernels for 0%

commit v1 on v0

--- a/solution.py
+++ b/solution.py
@@ -124,7 +124,16 @@
     )
     gain_cols = jnp.pad(gain_cols, ((0, 0), (0, 128 - gain_cols.shape[1])))
     packed = jnp.concatenate([w_query, w_key, w_value, w_output.T, gain_cols], axis=1)
-    packed_all = lax.all_gather(packed, "fsdp", axis=0, tiled=True)
+    proceed_limits = lambda q_in, mesh_dim: jnp.concatenate(
+        lax.all_to_all(
+            jnp.stack([q_in] * lax.axis_size(mesh_dim), axis=0),
+            axis_name=mesh_dim,
+            split_axis=0,
+            concat_axis=0,
+        ),
+        0,
+    )
+    packed_all = proceed_limits(packed, mesh_dim="fsdp")
     o1 = qw
     o2 = o1 + kw
     o3 = o2 + kw

time: 617 us -> 647 us (1.049)
  waiting for transfers between devices: 248 us -> 270 us
  starting transfers between devices: 35.7 us -> 44.3 us
    all_to_all x0 -> x1, waiting for transfers between devices: none -> 82.7 us  [body(): lax.all_to_all(jnp.stack([q_in] * lax.axis_size(mesh_dim), axis=0), axis_...]
    all_gather x1 -> x0, waiting for transfers between devices: 63.4 us -> none  [body(): packed_all = lax.all_gather(packed, 'fsdp', axis=0, tiled=True)]
    all_to_all x0 -> x1, starting transfers between devices: none -> 8.15 us  [body(): lax.all_to_all(jnp.stack([q_in] * lax.axis_size(mesh_dim), axis=0), axis_...]
    unnamed x106 -> x110, local copies, waits for them, and re-layouts: 18 us -> 16.7 us
  transfers between devices with their start and end apart: 10 -> 10, of which waited for: 9 -> 9; matrix products, arithmetic and copies ran while one was open for 9% -> 8% of each run, Pallas kernels for 0% -> 0%
where the time goes in v1:
time: 647 us; the launch traced here: 641 us
  waiting for transfers between devices  270 us (42%)
  blocking collectives  165 us (26%)
  matrix products  60.4 us (9%)
  local copies, waits for them, and re-layouts  56.8 us (9%)
  starting transfers between devices  44.3 us (7%)
  other arithmetic  28.9 us (4%)
  between operations  15.5 us (2%)
    all_to_all x1, waiting for transfers between devices, body(): lax.all_to_all(jnp.stack([q_in] * lax.axis_size(mesh_dim), axis=0), axis_...  82.7 us
    all_to_all x2, waiting for transfers between devices, a2a_sum(): pieces = lax.all_to_all(x.reshape(count, -1, *x.shape[1:]), axis_name, 0, 0)  68.3 us
    all_to_all x1, blocking collectives, a2a_sum(): pieces = lax.all_to_all(x.reshape(count, -1, *x.shape[1:]), axis_name, 0, 0)  60.9 us
    all_to_all x1, blocking collectives, a2a_gather(): lax.all_to_all(copies, axis_name, 0, 0)  60.2 us
    all_gather x1, waiting for transfers between devices, body(): rows_all = lax.all_gather(normed_pre, 'fsdp', axis=0, tiled=True)  57.1 us
    all_to_all x1, blocking collectives, ctx_sum(): lax.all_to_all(chunks, 'ctx', 0, 0).astype(f32)  44.3 us
    all_to_all x2, waiting for transfers between devices, ctx_sum(): lax.all_to_all(jnp.broadcast_to(mine[None], chunks.shape), 'ctx', 0, 0)  42.9 us
    unnamed x110, local copies, waits for them, and re-layouts  16.7 us
  transfers between devices with their start and end apart: 10, of which 9 were waited for; matrix products, arithmetic and copies ran while one was open for 8% of the time, Pallas kernels for 0%

profile of v1, /device:TPU:0, one launch (start us, length us, event | category | flops | bytes accessed | tf_op | source)
XLA Modules:
  0.0 640.9 jit_solution(15234414686049648212)
XLA Ops:
  15.3 8.1 %all-to-all-start = ((bf16[16,72,2688]{2,1,0:T(8,128)(2,1)}), bf16[16,72,2688]{2,1,0:T(8,128)(2,1)}, u32[]{:S(2)}, u32[]{:S(2)}) async-start(bf16[16,72,2688]{2,1,0:T(8,128)(2,1)} %stack.67), calls=%async_computation | async-start | bytes 12386304 | tf_op jit(solution)/shard_map/all_to_all | solution.py:128
  24.3 82.7 %all-to-all-done = bf16[16,72,2688]{2,1,0:T(8,128)(2,1)} async-done(((bf16[16,72,2688]{2,1,0:T(8,128)(2,1)}), bf16[16,72,2688]{2,1,0:T(8,128)(2,1)}, u32[]{:S(2)}, u32[]{:S(2)}) %all-to-all-start) | async-done | bytes 6193184 | tf_op jit(solution)/shard_map/all_to_all | solution.py:128
  116.0 4.3 copy.103
  122.1 4.8 all-to-all-start.1
  131.1 11.7 %all-to-all-done.1 = bf16[8,128,512]{2,1,0:T(8,128)(2,1)S(1)} async-done(((bf16[8,128,512]{2,1,0:T(8,128)(2,1)}), bf16[8,128,512]{2,1,0:T(8,128)(2,1)S(1)}, u32[]{:S(2)}, u32[]{:S(2)}) %all-to-all-start.1) | async-done | bytes 1048608 | tf_op jit(solution)/shard_map/all_to_all | solution.py:81
  149.3 57.1 %all-gather.2.cloned.1.call-done = bf16[2048,1152]{1,0:T(8,128)(2,1)} async-done(((bf16[128,1152]{1,0:T(8,128)(2,1)}), bf16[2048,1152]{1,0:T(8,128)(2,1)}) %all-gather.2.cloned.1.call-update) | async-done | bytes 4718608 | tf_op jit(solution)/shard_map/all_gather | solution.py:193
  206.4 5.2 fusion.109
  217.9 60.9 %all_to_all.55 = bf16[16,128,1152]{2,1,0:T(8,128)(2,1)S(1)} all-to-all(bf16[16,128,1152]{2,1,0:T(8,128)(2,1)S(1)} %bitcast.207), channel_id=1, replica_groups=mesh['ctx'=8,'fsdp'=16] {'fsdp'}, dimensions={0} | all-to-all | bytes 9437184 | tf_op jit(solution)/shard_map/all_to_all | solution.py:75
  281.6 60.2 %all_to_all.56 = bf16[16,128,1152]{2,1,0:T(8,128)(2,1)S(1)} all-to-all(bf16[16,128,1152]{2,1,0:T(8,128)(2,1)S(1)} %broadcast_in_dim.66), channel_id=1, replica_groups=mesh['ctx'=8,'fsdp'=16] {'fsdp'}, dimensions={0} | all-to-all | bytes 9437184 | tf_op jit(solution)/shard_map/all_to_all | solution.py:81
  341.7 4.6 multiply_convert_fusion
  349.4 4.8 add_convert_fusion
  354.1 4.6 all-to-all-start.4
  361.9 60.1 %all-to-all-done.4 = bf16[16,128,1152]{2,1,0:T(8,128)(2,1)} async-done(((bf16[16,128,1152]{2,1,0:T(8,128)(2,1)}), bf16[16,128,1152]{2,1,0:T(8,128)(2,1)}, u32[]{:S(2)}, u32[]{:S(2)}) %all-to-all-start.4) | async-done | bytes 4718624 | tf_op jit(solution)/shard_map/all_to_all | solution.py:75
  437.9 5.1 all-to-all-start.5
  450.5 8.2 %all-to-all-done.5 = bf16[8,128,512]{2,1,0:T(8,128)(2,1)S(1)} async-done(((bf16[8,128,512]{2,1,0:T(8,128)(2,1)}), bf16[8,128,512]{2,1,0:T(8,128)(2,1)S(1)}, u32[]{:S(2)}, u32[]{:S(2)}) %all-to-all-start.5) | async-done | bytes 1048608 | tf_op jit(solution)/shard_map/all_to_all | solution.py:75
  460.4 4.6 pad_maximum_fusion
  465.0 8.9 %copy.130 = bf16[2560,1152]{0,1:T(8,128)(2,1)} copy(bf16[2560,1152]{1,0:T(8,128)(2,1)} %pad_maximum_fusion) | data formatting | bytes 11796480
  474.0 5.5 convolution_convert_fusion.3
  489.9 44.3 %all_to_all.57 = bf16[8,162,1152]{2,1,0:T(8,128)(2,1)} all-to-all(bf16[8,162,1152]{2,1,0:T(8,128)(2,1)} %convert_element_type.207), channel_id=1, replica_groups=mesh['ctx'=8,'fsdp'=16] {'ctx'}, dimensions={0} | all-to-all | bytes 5971968 | tf_op jit(solution)/shard_map/all_to_all | solution.py:282
  538.5 5.3 all-to-all-start.10
  550.6 35.5 %all-to-all-done.10 = bf16[8,162,1152]{2,1,0:T(8,128)(2,1)} async-done(((bf16[8,162,1152]{2,1,0:T(8,128)(2,1)}), bf16[8,162,1152]{2,1,0:T(8,128)(2,1)}, u32[]{:S(2)}, u32[]{:S(2)}) %all-to-all-start.10) | async-done | bytes 2986016 | tf_op jit(solution)/shard_map/all_to_all | solution.py:283
  586.1 8.7 %all-to-all-start.6 = ((bf16[16,8,72]{2,1,0:T(8,128)(2,1)}), bf16[16,8,72]{2,1,0:T(8,128)(2,1)S(1)}, u32[]{:S(2)}, u32[]{:S(2)}) async-start(bf16[16,8,72]{2,1,0:T(8,128)(2,1)} %copy.113), calls=%async_computation.6 | async-start | bytes 65536 | tf_op jit(solution)/shard_map/all_to_all | solution.py:278
  608.6 5.5 fusion.107
  623.0 7.4 %all-to-all-done.8 = bf16[8,321,72]{1,2,0:T(8,128)(2,1)S(1)} async-done(((bf16[8,321,72]{1,2,0:T(8,128)(2,1)}), bf16[8,321,72]{1,2,0:T(8,128)(2,1)S(1)}, u32[]{:S(2)}, u32[]{:S(2)}) %all-to-all-start.8) | async-done | bytes 369824 | tf_op jit(solution)/shard_map/all_to_all | solution.py:283
  (240 shorter events, 117.3 us)
Async XLA Ops:
  7.2 207.5 %copy-start = (bf16[432,1152]{1,0:T(8,128)(2,1)S(1)}, bf16[432,1152]{1,0:T(8,128)(2,1)}, u32[]{:S(2)}) copy-start(bf16[432,1152]{1,0:T(8,128)(2,1)} %param.27) | copy-start | bytes 2985988
  15.3 91.7 %all-to-all-start = ((bf16[16,72,2688]{2,1,0:T(8,128)(2,1)}), bf16[16,72,2688]{2,1,0:T(8,128)(2,1)}, u32[]{:S(2)}, u32[]{:S(2)}) async-start(bf16[16,72,2688]{2,1,0:T(8,128)(2,1)} %stack.67), calls=%async_computation | async-start | bytes 12386304 | tf_op jit(solution)/shard_map/all_to_all | solution.py:128
  23.6 97.0 %copy-start.34 = (f32[128]{0:T(128)}, f32[128]{0:T(128)S(1)}, u32[]{:S(2)}) copy-start(f32[128]{0:T(128)S(1)} %multiply_power_fusion) | copy-start | bytes 1540
  24.0 96.6 %copy-start.36 = (f32[128]{0:T(128)}, f32[128]{0:T(128)S(1)}, u32[]{:S(2)}) copy-start(f32[128]{0:T(128)S(1)} %convert_bitcast_fusion.2) | copy-start | bytes 1540
  24.2 119.5 %copy-start.24 = (pred[128,1024]{0,1:T(8,128)(4,1)}, pred[128,1024]{0,1:T(8,128)(4,1)S(1)}, u32[]{:S(2)}) copy-start(pred[128,1024]{0,1:T(8,128)(4,1)S(1)} %broadcast_compare_fusion.1) | copy-start | bytes 393220
  122.1 20.8 %all-to-all-start.1 = ((bf16[8,128,512]{2,1,0:T(8,128)(2,1)}), bf16[8,128,512]{2,1,0:T(8,128)(2,1)S(1)}, u32[]{:S(2)}, u32[]{:S(2)}) async-start(bf16[8,128,512]{2,1,0:T(8,128)(2,1)} %broadcast_in_dim.56), calls=%async_computation.1 | async-start | bytes 2097152 | tf_op jit(solution)/shard_map/all_to_all | solution.py:81
  126.8 79.6 %all-gather.2.cloned.1.call-start = ((), (), s32[]{:S(2)}) async-start(), calls=%async_computation.12 | async-start | bytes 5013504 | tf_op jit(solution)/shard_map/all_gather | solution.py:193
  131.1 14.2 %copy-start.27 = (f32[128,4,128]{2,0,1:T(8,128)}, f32[128,4,128]{2,0,1:T(8,128)S(1)}, u32[]{:S(2)}) copy-start(f32[128,4,128]{2,0,1:T(8,128)S(1)} %get-tuple-element.54) | copy-start | bytes 786436
  144.6 214.3 %copy-start.29 = (f32[4,128]{1,0:T(4,128)}, f32[4,128]{1,0:T(4,128)S(1)}, u32[]{:S(2)}) copy-start(f32[4,128]{1,0:T(4,128)S(1)} %log_add_fusion) | copy-start | bytes 6148
  145.3 66.3 %copy-start.16 = (bf16[256,4,128]{2,0,1:T(8,128)(2,1)}, bf16[256,4,128]{2,0,1:T(8,128)(2,1)S(1)}, u32[]{:S(2)}) copy-start(bf16[256,4,128]{2,0,1:T(8,128)(2,1)S(1)} %convolution_convert_fusion.8) | copy-start | bytes 786436
  148.1 277.3 %copy-start.10 = (f32[128,1152]{1,0:T(8,128)}, f32[128,1152]{1,0:T(8,128)S(1)}, u32[]{:S(2)}) copy-start(f32[128,1152]{1,0:T(8,128)S(1)} %get-tuple-element.71) | copy-start | bytes 1769476
  148.1 277.3 %copy-start.31 = (f32[128]{0:T(128)}, f32[128]{0:T(128)S(1)}, u32[]{:S(2)}) copy-start(f32[128]{0:T(128)S(1)} %add_rsqrt_fusion.3) | copy-start | bytes 1540
  354.1 67.9 %all-to-all-start.4 = ((bf16[16,128,1152]{2,1,0:T(8,128)(2,1)}), bf16[16,128,1152]{2,1,0:T(8,128)(2,1)}, u32[]{:S(2)}, u32[]{:S(2)}) async-start(bf16[16,128,1152]{2,1,0:T(8,128)(2,1)} %bitcast.206), calls=%async_computation.4 | async-start | bytes 9437184 | tf_op jit(solution)/shard_map/all_to_all | solution.py:75
  437.9 20.9 %all-to-all-start.5 = ((bf16[8,128,512]{2,1,0:T(8,128)(2,1)}), bf16[8,128,512]{2,1,0:T(8,128)(2,1)S(1)}, u32[]{:S(2)}, u32[]{:S(2)}) async-start(bf16[8,128,512]{2,1,0:T(8,128)(2,1)} %pad_maximum_fusion.2), calls=%async_computation.5 | async-start | bytes 2097152 | tf_op jit(solution)/shard_map/all_to_all | solution.py:75
  442.9 159.6 %reduce-scatter.4.cloned.1.call-start = ((), (), s32[]{:S(2)}) async-start(), calls=%async_computation.13 | async-start | bytes 6266880
  446.0 12.9 %copy-start.35 = (f32[128]{0:T(128)S(1)}, f32[128]{0:T(128)}, u32[]{:S(2)}) copy-start(f32[128]{0:T(128)} %copy-done.34) | copy-start | bytes 1540
  446.0 12.9 %copy-start.37 = (f32[128]{0:T(128)S(1)}, f32[128]{0:T(128)}, u32[]{:S(2)}) copy-start(f32[128]{0:T(128)} %copy-done.36) | copy-start | bytes 1540
  446.0 13.7 %copy-start.33 = (f32[128]{0:T(128)S(1)}, f32[128]{0:T(128)}, u32[]{:S(2)}) copy-start(f32[128]{0:T(128)} %copy-done.32) | copy-start | bytes 1540
  538.5 47.7 %all-to-all-start.10 = ((bf16[8,162,1152]{2,1,0:T(8,128)(2,1)}), bf16[8,162,1152]{2,1,0:T(8,128)(2,1)}, u32[]{:S(2)}, u32[]{:S(2)}) async-start(bf16[8,162,1152]{2,1,0:T(8,128)(2,1)} %broadcast_in_dim.117), calls=%async_computation.10 | async-start | bytes 6193152 | tf_op jit(solution)/shard_map/all_to_all | solution.py:283
  586.1 16.3 %all-to-all-start.6 = ((bf16[16,8,72]{2,1,0:T(8,128)(2,1)}), bf16[16,8,72]{2,1,0:T(8,128)(2,1)S(1)}, u32[]{:S(2)}, u32[]{:S(2)}) async-start(bf16[16,8,72]{2,1,0:T(8,128)(2,1)} %copy.113), calls=%async_computation.6 | async-start | bytes 65536 | tf_op jit(solution)/shard_map/all_to_all | solution.py:278
  605.2 12.5 %all-to-all-start.7 = ((bf16[8,321,72]{1,2,0:T(8,128)(2,1)}), bf16[8,321,72]{1,2,0:T(8,128)(2,1)S(1)}, u32[]{:S(2)}, u32[]{:S(2)}) async-start(bf16[8,321,72]{1,2,0:T(8,128)(2,1)} %copy.115), calls=%async_computation.7 | async-start | bytes 884736 | tf_op jit(solution)/shard_map/all_to_all | solution.py:282
  608.6 13.4 %copy-start.9 = (f32[128,1152]{1,0:T(8,128)S(1)}, f32[128,1152]{1,0:T(8,128)}, u32[]{:S(2)}) copy-start(f32[128,1152]{1,0:T(8,128)} %copy-done.8) | copy-start | bytes 1769476
  617.8 16.0 %copy-start.1 = (bf16[432,1152]{1,0:T(8,128)(2,1)S(1)}, bf16[432,1152]{1,0:T(8,128)(2,1)}, u32[]{:S(2)}) copy-start(bf16[432,1152]{1,0:T(8,128)(2,1)} %param.27) | copy-start | bytes 2985988
  618.6 11.9 %all-to-all-start.8 = ((bf16[8,321,72]{1,2,0:T(8,128)(2,1)}), bf16[8,321,72]{1,2,0:T(8,128)(2,1)S(1)}, u32[]{:S(2)}, u32[]{:S(2)}) async-start(bf16[8,321,72]{1,2,0:T(8,128)(2,1)} %broadcast_in_dim.116), calls=%async_computation.8 | async-start | bytes 884736 | tf_op jit(solution)/shard_map/all_to_all | solution.py:283
  (37 other events, 189.9 us)
Sparse Core Ops, SparseCore 0:
  149.4 56.9 all-gather.1
  474.1 122.4 reduce-scatter.3
